TPU v7x, 32 devices: a whole 2x2x4 slice. The times are simulated.
32 devices in a mesh: fourier: 8 (over y, x, core), mer: 4 (over z).
Axes of the slice: x: 2, y: 2, z: 4, core: 2. Of those that a mesh axis runs over, the one named last changes fastest.
Arguments:
- velocity: float32 [3, 256, 64, 1024], P(None, 'fourier', None, 'mer')
- metrics: float32 [4, 64, 1024], P(None, None, 'mer'), may hold values from -0.3 to 0.3
- lumped_mass: float32 [64, 1024], P(None, 'mer'), may hold values from 0.5 to 2
- element_ops: float32 [64, 64, 1024], P(None, None, 'mer'), may hold values from -0.75 to 0.75
- boundary_map: int32 [1024, 28], P('mer'), may hold values from 0 to 13311, as said below
- block_cols: int32 [104, 4], P('mer'), may hold values from 0 to 103, as said below
- schur_blocks: float32 [104, 4, 128, 128], P('mer'), may hold values from -0.25 to 0.25
Outputs:
- element_out: float32 [3, 256, 64, 1024], P(None, 'fourier', None, 'mer')
- boundary_out: float32 [3, 256, 13312], P(None, 'fourier', 'mer')
Inputs may be any that keep to these rules, and one draw needn't show every extreme that they name: `boundary_map`: every entry of an element of slab s (elements s * 256 to (s + 1) * 256 - 1) lies from s * 3328 to (s + 1) * 3328 + 127, and for the last slab below (s + 1) * 3328; both ends are taken in every slab. `block_cols`: entry s of row r differs from r by at most 2; entry 0 is r itself.
All inputs are finite; a program needn't handle non-finite values.
Results may differ from a plain program's by a relative error of at most 0.00014.
Values sent between devices are 32-bit elements; how exact they have to be, the bound alone decides.
No kernel may reach another device: no remote copies, remote signals or barrier semaphores. Data moves between devices by JAX's collectives and lax.ppermute only.
A program may use at most 192 MiB of HBM per device.

v0:
```python
import jax
import jax.numpy as jnp
import numpy as np
from jax import lax
from jax.sharding import PartitionSpec as P

PERIM = 28
K = 256
HB = 2
gauss_nodes = [
    -1.0,
    -0.8717401485096066,
    -0.5917001814331423,
    -0.2092992179024789,
    0.2092992179024789,
    0.5917001814331423,
    0.8717401485096066,
    1.0,
]
wave_scale = 1.0 / 32.0


def passed_along(value, axis, by):
    count = lax.axis_size(axis)
    pairs = [(i, i + by) for i in range(count) if 0 <= i + by < count]
    return lax.ppermute(value, axis, pairs)


def padded(value, sides, width):
    for axis, dim in sides:
        count, length = (lax.axis_size(axis), value.shape[dim])
        up = [(i, (i + 1) % count) for i in range(count - 1)]
        down = [(j, i) for i, j in up]
        last = lax.slice_in_dim(value, length - width, length, axis=dim)
        leading = lax.slice_in_dim(value, 0, width, axis=dim)
        before = lax.ppermute(last, axis, up)
        after = lax.ppermute(leading, axis, down)
        value = jnp.concatenate([before, value, after], axis=dim)
    return value


def node_tables():
    nodes = np.array(gauss_nodes)
    count = nodes.shape[0]
    barycentric = np.array(
        [1.0 / np.prod([nodes[i] - nodes[k] for k in range(count) if k != i]) for i in range(count)]
    )
    matrix = np.zeros((count, count))
    for i in range(count):
        for j in range(count):
            if i != j:
                matrix[i, j] = barycentric[j] / barycentric[i] / (nodes[i] - nodes[j])
        matrix[i, i] = -np.sum(matrix[i])
    return (np.kron(matrix, np.eye(count)), np.kron(np.eye(count), matrix))


def perimeter_points():
    points = [8 * a + b for a in range(8) for b in range(8) if a in (0, 7) or b in (0, 7)]
    return np.array(points, dtype=np.int32)


def spectral_tables(modes):
    planes = 3 * modes // 2
    index = np.arange(modes)
    wave = np.where(index == modes - 1, modes // 2, (index + 1) // 2)
    is_sine = (index % 2 == 0) & (index > 0) & (index < modes - 1)
    theta = 2.0 * np.pi * np.arange(planes) / planes
    angle = theta[:, None] * wave[None, :]
    basis = np.where(is_sine[None, :], np.sin(angle), np.cos(angle))
    deriv = wave_scale * wave[None, :] * np.where(is_sine[None, :], np.cos(angle), -np.sin(angle))
    weight = np.where(index == 0, 1.0, 2.0) / planes
    back = (basis * weight[None, :]).T
    return (basis, deriv, back, wave)


def per_device(velocity, metrics, lumped_mass, element_ops, boundary_map, block_cols, schur_blocks):
    high = lax.Precision.HIGHEST
    modes = velocity.shape[1]
    elems = velocity.shape[3]
    groups = lax.axis_size("fourier")
    sub_elems = elems // groups
    part = lax.axis_index("fourier")
    slab = lax.axis_index("mer")
    block_rows = schur_blocks.shape[0]
    block_size = schur_blocks.shape[2]
    owned_count = block_rows * block_size
    basis, deriv, back, wave = spectral_tables(K)
    forward_table = jnp.asarray(basis, jnp.float32)
    deriv_table = jnp.asarray(deriv, jnp.float32)
    back_table = jnp.asarray(back, jnp.float32)
    deriv_r_np, deriv_s_np = node_tables()
    deriv_r = jnp.asarray(deriv_r_np, jnp.float32)
    deriv_s = jnp.asarray(deriv_s_np, jnp.float32)
    incoming = lax.all_to_all(velocity, "fourier", split_axis=3, concat_axis=1, tiled=True)
    physical = jnp.einsum("jk,fkpe->fjpe", forward_table, incoming, precision=high)
    planes = physical[:3]
    grad_z = jnp.einsum("jk,fkpe->fjpe", deriv_table, incoming, precision=high)
    local_metrics = lax.dynamic_slice_in_dim(metrics, part * sub_elems, sub_elems, 2)
    along_r = jnp.einsum("qp,fjpe->fjqe", deriv_r, planes, precision=high)
    along_s = jnp.einsum("qp,fjpe->fjqe", deriv_s, planes, precision=high)
    grad_x = local_metrics[0] * along_r + local_metrics[2] * along_s
    grad_y = local_metrics[1] * along_r + local_metrics[3] * along_s
    advection = -(planes[0:1] * grad_x + planes[1:2] * grad_y + planes[2:3] * grad_z)
    projected = jnp.einsum("kj,fjpe->fkpe", back_table, advection, precision=high)
    returned = lax.all_to_all(projected, "fourier", split_axis=1, concat_axis=3, tiled=True)
    forcing = velocity + returned
    wave_all = jnp.asarray(wave, jnp.float32)
    local_wave = lax.dynamic_slice_in_dim(wave_all, part * modes, modes)
    helm = 1.0 + 4.0 * (local_wave / (K / 2)) ** 2
    element_out = jnp.einsum("ije,fkje->fkie", element_ops, forcing, precision=high)
    element_out = element_out + helm[None, :, None, None] * lumped_mass[None, None] * forcing
    perim = perimeter_points()
    values = element_out[:, :, perim, :]
    values = jnp.transpose(values, (3, 2, 0, 1)).reshape(elems * PERIM, 3 * modes)
    local_ids = boundary_map.reshape(-1) - slab * owned_count
    partial_sums = jax.ops.segment_sum(values, local_ids, num_segments=owned_count + block_size)
    partial_sums = partial_sums.T.reshape(3, modes, owned_count + block_size)
    reach_rows = HB * block_size
    owned = partial_sums[:, :, :owned_count]
    shared = partial_sums[:, :, owned_count:]
    arrived = passed_along(shared, "mer", 1)
    owned = owned.at[:, :, :block_size].add(arrived)
    extended = padded(owned, (("mer", 2),), reach_rows)
    blocked = extended.reshape(3 * modes, block_rows + 2 * HB, block_size)
    local_cols = block_cols - slab * block_rows + HB
    picked = blocked[:, local_cols, :]
    result = jnp.einsum("rsab,frsb->fra", schur_blocks, picked, precision=high)
    boundary_out = result.reshape(3, modes, owned_count)
    return (element_out, boundary_out)


def solution(mesh):
    in_specs = (
        P(None, "fourier", None, "mer"),
        P(None, None, "mer"),
        P(None, "mer"),
        P(None, None, "mer"),
        P("mer", None),
        P("mer", None),
        P("mer", None, None, None),
    )
    out_specs = (P(None, "fourier", None, "mer"), P(None, "fourier", "mer"))
    return jax.shard_map(
        per_device, mesh=mesh, in_specs=in_specs, out_specs=out_specs, check_vma=False
    )
```

profile of v0, /device:TPU:0, one launch (start us, length us, event | category | flops | bytes accessed | tf_op | source)
XLA Modules:
  0.0 565.5 jit_solution(6990238287051673647)
XLA Ops:
  0.6 12.7 %copy.110 = f32[3,32,64,256]{2,1,0,3:T(8,128)} copy(f32[3,32,64,256]{3,2,1,0:T(8,128)} %param.17) | data formatting | bytes 12582912 | tf_op args[0]
  13.4 12.6 %reshape.114 = f32[8,1,196608]{2,1,0:T(1,128)} reshape(f32[256,3,32,64]{3,2,1,0:T(8,128)} %bitcast.101) | data formatting | bytes 12582912
  26.0 5.3 all-to-all-start
  31.5 0.7 copy.103
  32.2 0.7 copy.102
  32.9 0.7 copy.101
  33.5 69.6 %all-to-all-done = f32[8,1,196608]{2,1,0:T(1,128)} async-done(((f32[8,1,196608]{2,1,0:T(1,128)}), f32[8,1,196608]{2,1,0:T(1,128)}, u32[]{:S(2)}, u32[]{:S(2)}) %all-to-all-start) | async-done | bytes 6291488 | tf_op jit(solution)/shard_map/all_to_all | solution.py:94
  103.2 0.6 broadcast.68
  103.7 19.7 %reduce.2 = f32[8,196608]{1,0:T(8,128)} reduce(f32[8,1,196608]{2,1,0:T(1,128)} %all-to-all-done, f32[]{:T(128)} %broadcast.68), dimensions={1}, to_apply=%all_to_all.26.reduce_sub_computation | reduce | bytes 12582916 | tf_op jit(solution)/shard_map/all_to_all | solution.py:94
  123.4 12.2 %reshape.115 = f32[256,3,32,64]{3,2,1,0:T(8,128)} reshape(f32[8,196608]{1,0:T(8,128)} %reduce.2) | data formatting | bytes 12582912
  135.6 20.4 %copy.99 = f32[3,8,32,64,32]{3,4,2,1,0:T(8,128)} copy(f32[3,8,32,64,32]{3,2,0,4,1:T(8,128)} %bitcast.104) | data formatting | bytes 12582912 | tf_op jit(solution)/shard_map/all_to_all | solution.py:94
  155.9 11.0 %copy.100 = f32[3,256,64,32]{1,2,3,0:T(8,128)} copy(f32[3,256,64,32]{2,3,1,0:T(8,128)} %bitcast.105) | data formatting | bytes 12582912 | tf_op jit(solution)/shard_map/all_to_all | solution.py:94
  167.0 13.4 %convolution_bitcast_fusion = f32[3,384,64,32]{1,2,3,0:T(8,128)S(1)} fusion(f32[384,256,1,1]{1,0,3,2:T(8,128)S(1)} %copy-done.3, f32[3,256,64,32]{1,2,3,0:T(8,128)} %copy.100), kind=kOutput, calls=%fused_computation.18 | convolution fusion | flops 7247757312 | bytes 16121856 | tf_op jit(solution)/shard_map/jk,fkpe->fjpe/dot_general | solution.py:95
  180.4 3.7 slice_bitcast_fusion.2
  184.1 2.9 copy-done
  186.9 11.4 %fusion.15 = f32[3,384,32,64]{1,3,2,0:T(8,128)} fusion(f32[3,384,64,32]{1,2,3,0:T(8,128)S(1)} %convolution_bitcast_fusion, f32[64,64,1,1]{1,0,3,2:T(8,128)S(1)} %copy-done.6), kind=kOutput, calls=%fused_computation.40 | convolution fusion | flops 1811939328 | bytes 18890752 | tf_op jit(solution)/shard_map/qp,fjpe->fjqe/dot_general | solution.py:99
  198.3 12.5 %fusion.16 = f32[384,3,64,32]{0,2,3,1:T(8,128)} fusion(f32[384,256,1,1]{1,0,3,2:T(8,128)S(1)} %copy-done.2, f32[3,256,64,32]{1,2,3,0:T(8,128)S(1)} %bitcast.103), kind=kOutput, calls=%fused_computation.41 | convolution fusion | flops 7247757312 | bytes 16121856 | tf_op jit(solution)/shard_map/jk,fkpe->fjpe/dot_general | solution.py:97
  210.8 21.6 %fusion = f32[3,384,64,32]{1,2,3,0:T(8,128)} fusion(f32[3,384,32,64]{1,3,2,0:T(8,128)} %fusion.15, f32[384,3,64,32]{0,2,3,1:T(8,128)} %fusion.16, f32[384,64,32]{0,1,2:T(8,128)} %get-tuple-element.25, f32[64,32]{0,1:T(8,128)S(1)} %copy.104, f32[64,32]{0,1:T(8,128)} %copy.103, f32[384,64,32]{0,1,2:T(8,128)} %get-tuple-element.26, f32[64,32]{0,1:T(8,128)} %copy.102, ...), kind=kOutput, calls=%fused_computation.6 | convolution fusion | flops 1840250880 | bytes 47235072 | tf_op jit(solution)/shard_map/qp,fjpe->fjqe/dot_general | solution.py:100
  232.5 20.0 %fusion.8 = f32[3,256,64,32]{1,3,2,0:T(8,128)} fusion(f32[256,384,1,1]{1,0,3,2:T(8,128)S(1)} %copy-done.1, f32[3,384,64,32]{1,2,3,0:T(8,128)} %fusion), kind=kOutput, calls=%fused_computation.22 | convolution fusion | flops 7247757312 | bytes 16121856 | tf_op jit(solution)/shard_map/kj,fjpe->fkpe/dot_general | solution.py:104
  252.5 12.8 %copy.107 = f32[3,256,64,32]{2,3,0,1:T(8,128)} copy(f32[3,256,64,32]{1,3,2,0:T(8,128)} %fusion.8) | data formatting | bytes 12582912 | tf_op jit(solution)/shard_map/kj,fjpe->fkpe/transpose | solution.py:104
  265.2 12.6 %reshape.116 = f32[8,1,196608]{2,1,0:T(1,128)} reshape(f32[256,3,32,64]{3,2,1,0:T(8,128)} %bitcast.106) | data formatting | bytes 12582912
  277.9 4.9 all-to-all-start.1
  283.0 9.2 %copy.127 = f32[64,64,256,1]{1,0,3,2:T(8,128)} copy(f32[64,64,256,1]{2,1,0,3:T(8,128)} %bitcast.114) | data formatting | bytes 8388608 | tf_op args[3]
  292.5 2.6 broadcast_multiply_fusion
  295.0 59.4 %all-to-all-done.1 = f32[8,1,196608]{2,1,0:T(1,128)} async-done(((f32[8,1,196608]{2,1,0:T(1,128)}), f32[8,1,196608]{2,1,0:T(1,128)}, u32[]{:S(2)}, u32[]{:S(2)}) %all-to-all-start.1) | async-done | bytes 6291488 | tf_op jit(solution)/shard_map/all_to_all | solution.py:105
  354.4 19.7 %reduce.3 = f32[8,196608]{1,0:T(8,128)} reduce(f32[8,1,196608]{2,1,0:T(1,128)} %all-to-all-done.1, f32[]{:T(128)} %broadcast.68), dimensions={1}, to_apply=%all_to_all.30.reduce_sub_computation | reduce | bytes 12582916 | tf_op jit(solution)/shard_map/all_to_all | solution.py:105
  374.1 12.3 %reshape.117 = f32[256,3,32,64]{3,2,1,0:T(8,128)} reshape(f32[8,196608]{1,0:T(8,128)} %reduce.3) | data formatting | bytes 12582912
  386.3 16.4 %copy.109 = f32[3,32,64,8,32]{2,1,0,4,3:T(8,128)} copy(f32[3,32,64,8,32]{2,4,0,1,3:T(8,128)} %bitcast.107) | data formatting | bytes 12582912 | tf_op jit(solution)/shard_map/all_to_all | solution.py:105
  402.7 14.6 %bitcast_add_fusion.1 = f32[3,32,64,256]{2,1,0,3:T(8,128)} fusion(f32[3,32,64,256]{2,1,0,3:T(8,128)} %copy.110, f32[3,32,64,8,32]{2,1,0,4,3:T(8,128)} %copy.109), kind=kLoop, calls=%fused_computation.4 | loop fusion | flops 1572864 | bytes 18874368 | tf_op jit(solution)/shard_map/add | solution.py:106
  417.3 25.5 %bitcast_add_fusion = f32[3,32,64,256]{2,1,0,3:T(8,128)} fusion(f32[3,32,64,256]{2,1,0,3:T(8,128)} %bitcast_add_fusion.1, f32[32,64,256]{1,0,2:T(8,128)} %broadcast_multiply_fusion, f32[64,64,256,1]{1,0,3,2:T(8,128)} %copy.127), kind=kOutput, calls=%fused_computation.3 | convolution fusion | flops 1211105280 | bytes 18874368 | tf_op jit(solution)/shard_map/ije,fkje->fkie/dot_general | solution.py:110
  442.9 12.1 %copy.114 = f32[3,32,64,256]{3,1,0,2:T(8,128)} copy(f32[3,32,64,256]{2,1,0,3:T(8,128)} %bitcast_add_fusion) | data formatting | bytes 12582912 | tf_op jit(solution)/shard_map/add | solution.py:111
  454.9 3.5 gather_fusion
  458.5 10.0 %copy.133 = f32[256,28,3,32]{3,2,1,0:T(4,128)} copy(f32[256,28,3,32]{0,3,2,1:T(8,128)S(1)} %bitcast.109) | data formatting | bytes 5505024 | tf_op jit(solution)/shard_map/reshape | solution.py:114
  468.4 14.7 %reshape.111 = f32[7168,96]{1,0:T(8,128)} reshape(f32[256,28,3,32]{3,2,1,0:T(4,128)} %copy.133) | data formatting | bytes 5505024 | tf_op jit(solution)/shard_map/reshape | solution.py:114
  483.1 39.3 %scatter_custom_fusion = f32[3456,96]{1,0:T(8,128)S(1)} fusion(s32[7168]{0:T(1024)S(1)} %reshape.95, f32[7168,96]{1,0:T(8,128)} %reshape.111, f32[]{:T(128)} %constant.71.clone.1), kind=kCustom, calls=%fused_computation.26 | custom fusion | flops 688128 | bytes 1327616 | tf_op jit(solution)/shard_map/scatter-add | solution.py:116
  522.5 0.5 copy.117
  523.0 4.4 collective-permute-start
  527.7 1.4 collective-permute-done
  529.1 1.5 collective-permute-start.2
  530.7 4.9 collective-permute-start.1
  535.6 11.0 %copy.121 = f32[3,32,64,256]{3,2,1,0:T(8,128)} copy(f32[3,32,64,256]{2,1,0,3:T(8,128)} %bitcast_add_fusion) | data formatting | bytes 12582912
  546.6 1.2 pad_maximum_fusion
  547.8 1.6 reshape.75
  549.4 0.9 copy.119
  550.3 3.1 gather_fusion.1
  553.4 9.8 %convolution_bitcast_fusion.1 = f32[96,26,128]{2,0,1:T(8,128)S(1)} fusion(f32[96,26,4,128]{3,0,2,1:T(8,128)} %bitcast.108, f32[26,4,128,128]{3,2,1,0:T(8,128)} %param.23), kind=kOutput, calls=%fused_computation.25 | convolution fusion | flops 1962934272 | bytes 13205504 | tf_op jit(solution)/shard_map/rsab,frsb->fra/dot_general | solution.py:127
  563.2 0.8 copy.120
  564.0 1.3 reshape.76
  (44 shorter events, 1.0 us)
Async XLA Ops:
  26.0 5.3 copy-start.5
  26.0 77.1 %all-to-all-start = ((f32[8,1,196608]{2,1,0:T(1,128)}), f32[8,1,196608]{2,1,0:T(1,128)}, u32[]{:S(2)}, u32[]{:S(2)}) async-start(f32[8,1,196608]{2,1,0:T(1,128)} %reshape.114), calls=%async_computation | async-start | bytes 12582912 | tf_op jit(solution)/shard_map/all_to_all | solution.py:94
  155.9 11.0 %copy-start.3 = (f32[384,256,1,1]{1,0,3,2:T(8,128)S(1)}, f32[384,256,1,1]{1,0,3,2:T(8,128)}, u32[]{:S(2)}) copy-start(f32[384,256,1,1]{1,0,3,2:T(8,128)} %constant.89) | copy-start | bytes 1179652
  180.3 6.6 %copy-start = (f32[3,384,64,32]{1,2,3,0:T(8,128)}, f32[3,384,64,32]{1,2,3,0:T(8,128)S(1)}, u32[]{:S(2)}) copy-start(f32[3,384,64,32]{1,2,3,0:T(8,128)S(1)} %convolution_bitcast_fusion) | copy-start | bytes 28311556
  180.4 6.6 %copy-start.6 = (f32[64,64,1,1]{1,0,3,2:T(8,128)S(1)}, f32[64,64,1,1]{1,0,3,2:T(8,128)}, u32[]{:S(2)}) copy-start(f32[64,64,1,1]{1,0,3,2:T(8,128)} %constant.90) | copy-start | bytes 49156
  180.4 17.9 %slice-start = ((s8[6291456]{0:T(1024)(128)(4,1)}), s8[4194304]{0:T(1024)(128)(4,1)S(1)}, s32[]{:S(2)}) async-start(s8[6291456]{0:T(1024)(128)(4,1)} %bitcast.102), calls=%async_computation.2 | async-start | bytes 8388608
  186.9 11.4 %slice-start.1 = ((s8[6291456]{0:T(1024)(128)(4,1)}), s8[2097152]{0:T(1024)(128)(4,1)S(1)}, s32[]{:S(2)}) async-start(s8[6291456]{0:T(1024)(128)(4,1)} %bitcast.102), calls=%async_computation.3 | async-start | bytes 4194304
  186.9 11.4 %copy-start.2 = (f32[384,256,1,1]{1,0,3,2:T(8,128)S(1)}, f32[384,256,1,1]{1,0,3,2:T(8,128)}, u32[]{:S(2)}) copy-start(f32[384,256,1,1]{1,0,3,2:T(8,128)} %constant.92) | copy-start | bytes 1179652
  210.8 21.7 %copy-start.1 = (f32[256,384,1,1]{1,0,3,2:T(8,128)S(1)}, f32[256,384,1,1]{1,0,3,2:T(8,128)}, u32[]{:S(2)}) copy-start(f32[256,384,1,1]{1,0,3,2:T(8,128)} %constant.93) | copy-start | bytes 1179652
  277.9 5.0 copy-start.4
  277.9 76.5 %all-to-all-start.1 = ((f32[8,1,196608]{2,1,0:T(1,128)}), f32[8,1,196608]{2,1,0:T(1,128)}, u32[]{:S(2)}, u32[]{:S(2)}) async-start(f32[8,1,196608]{2,1,0:T(1,128)} %reshape.116), calls=%async_computation.1 | async-start | bytes 12582912 | tf_op jit(solution)/shard_map/all_to_all | solution.py:105
  282.9 9.2 %copy-start.7 = (s32[256,28]{0,1:T(8,128)S(1)}, s32[256,28]{0,1:T(8,128)}, u32[]{:S(2)}) copy-start(s32[256,28]{0,1:T(8,128)} %param.21) | copy-start | bytes 86020
  282.9 9.4 %copy-start.10 = (f32[256]{0:T(256)S(1)}, f32[256]{0:T(256)}, u32[]{:S(2)}) copy-start(f32[256]{0:T(256)} %constant.82.clone) | copy-start | bytes 3076
  283.0 9.5 %copy-start.9 = (s32[28]{0:T(128)S(1)}, s32[28]{0:T(128)}, u32[]{:S(2)}) copy-start(s32[28]{0:T(128)} %constant.88) | copy-start | bytes 340
  468.4 58.9 %copy-start.8 = (s32[26,4]{0,1:T(4,128)S(1)}, s32[26,4]{0,1:T(4,128)}, u32[]{:S(2)}) copy-start(s32[26,4]{0,1:T(4,128)} %param.22) | copy-start | bytes 1252
  523.0 6.1 %collective-permute-start = (f32[3,32,128]{2,1,0:T(8,128)S(1)}, f32[3,32,128]{2,1,0:T(8,128)S(1)}, u32[]{:S(2)}, u32[]{:S(2)}) collective-permute-start(f32[3,32,128]{2,1,0:T(8,128)S(1)} %slice.79), channel_id=1, source_target_pairs={{0,1},{1,2},{2,3},{4,5},{5,6},{6,7},{8,9},{9,10},{10,11},{12,13},{... | collective-permute-start | bytes 147464 | tf_op jit(solution)/shard_map/ppermute | solution.py:26
  529.1 17.4 %collective-permute-start.2 = (f32[3,32,256]{2,1,0:T(8,128)S(1)}, f32[3,32,256]{2,1,0:T(8,128)S(1)}, u32[]{:S(2)}, u32[]{:S(2)}) collective-permute-start(f32[3,32,256]{2,1,0:T(8,128)S(1)} %get-tuple-element.28), channel_id=1, source_target_pairs={{1,0},{2,1},{3,2},{5,4},{6,5},{7,6},{9,8},{10,9},{11,10},{13,12},{... | collective-permute-start | bytes 294920 | tf_op jit(solution)/shard_map/ppermute | solution.py:37
  530.7 15.9 %collective-permute-start.1 = (f32[3,32,256]{2,1,0:T(8,128)S(1)}, f32[3,32,256]{2,1,0:T(8,128)S(1)}, u32[]{:S(2)}, u32[]{:S(2)}) collective-permute-start(f32[3,32,256]{2,1,0:T(8,128)S(1)} %get-tuple-element.27), channel_id=1, source_target_pairs={{0,1},{1,2},{2,3},{4,5},{5,6},{6,7},{8,9},{9,10},{10,11},{12,13},{... | collective-permute-start | bytes 294920 | tf_op jit(solution)/shard_map/ppermute | solution.py:36
where the time goes:
time: 571 us; the launch traced here: 566 us
  local copies, waits for them, and re-layouts  202 us (35%)
  waiting for transfers between devices  130 us (23%)
  matrix products  114 us (20%)
  other arithmetic  97.2 us (17%)
  starting transfers between devices  21 us (4%)
    unnamed x34, local copies, waits for them, and re-layouts  85.6 us
    all_to_all x1, waiting for transfers between devices, per_device(): lax.all_to_all(velocity, 'fourier', split_axis=3, concat_axis=1, tiled=True)  69.6 us
    all_to_all x1, waiting for transfers between devices, per_device(): lax.all_to_all(projected, 'fourier', split_axis=1, concat_axis=3, tiled=T...  59.4 us
    scatter-add x1, other arithmetic, per_device(): jax.ops.segment_sum(values, local_ids, num_segments=owned_count + block_s...  39.3 us
    all_to_all x3, local copies, waits for them, and re-layouts, per_device(): lax.all_to_all(velocity, 'fourier', split_axis=3, concat_axis=1, tiled=True)  32 us
    dot_general x1, matrix products, per_device(): jnp.einsum('ije,fkje->fkie', element_ops, forcing, precision=high)  25.5 us
    reshape x2, local copies, waits for them, and re-layouts, per_device(): jnp.transpose(values, (3, 2, 0, 1)).reshape(elems * PERIM, 3 * modes)  24.7 us
    dot_general x1, matrix products, per_device(): along_s = jnp.einsum('qp,fjpe->fjqe', deriv_s, planes, precision=high)  21.6 us
  transfers between devices with their start and end apart: 5, of which 3 were waited for; matrix products, arithmetic and copies ran while one was open for 5% of the time, Pallas kernels for 0%

commit v1 on v0

--- a/solution.py
+++ b/solution.py
@@ -3,6 +3,7 @@
 import numpy as np
 from jax import lax
 from jax.sharding import PartitionSpec as P
+from jax.lax import axis_index, ppermute, psum
 
 PERIM = 28
 K = 256
@@ -102,7 +103,25 @@
     grad_y = local_metrics[1] * along_r + local_metrics[3] * along_s
     advection = -(planes[0:1] * grad_x + planes[1:2] * grad_y + planes[2:3] * grad_z)
     projected = jnp.einsum("kj,fjpe->fkpe", back_table, advection, precision=high)
-    returned = lax.all_to_all(projected, "fourier", split_axis=1, concat_axis=3, tiled=True)
+    latest = psum(1, axis_name="fourier")
+    res = axis_index("fourier")
+    n_now, v_next = (latest, res)
+    v_now = list(projected.shape)
+    local_next = projected.shape[1] // n_now
+    v_now[1] = local_next
+    earlier = v_now[3]
+    v_now[3] = earlier * n_now
+    returned = jnp.zeros(v_now, projected.dtype)
+    for src_i in range(n_now):
+        placed = lax.dynamic_slice_in_dim(
+            projected, (v_next ^ src_i) * local_next, local_next, axis=1
+        )
+        if src_i:
+            x_next = tuple(((ii, ii ^ src_i) for ii in range(n_now)))
+            placed = ppermute(placed, axis_name="fourier", perm=x_next)
+        returned = lax.dynamic_update_slice_in_dim(
+            returned, placed, (v_next ^ src_i) * earlier, axis=3
+        )
     forcing = velocity + returned
     wave_all = jnp.asarray(wave, jnp.float32)
     local_wave = lax.dynamic_slice_in_dim(wave_all, part * modes, modes)

time: 571 us -> 602 us (1.054)
  waiting for transfers between devices: 130 us -> 174 us
  other arithmetic: 97.2 us -> 63 us
  local copies, waits for them, and re-layouts: 202 us -> 214 us
  matrix products: 114 us -> 124 us
    ppermute x0 -> x7, waiting for transfers between devices: none -> 101 us  [per_device(): placed = ppermute(placed, axis_name='fourier', perm=x_next)]
    all_to_all x1 -> x0, waiting for transfers between devices: 59.4 us -> none  [per_device(): lax.all_to_all(projected, 'fourier', split_axis=1, concat_axis=3, tiled=T...]
    dynamic_slice x0 -> x9, local copies, waits for them, and re-layouts: none -> 39.4 us  [per_device(): lax.dynamic_slice_in_dim(projected, (v_next ^ src_i) * local_next, local_...]
    unnamed x34 -> x44, local copies, waits for them, and re-layouts: 85.6 us -> 61.2 us
    dynamic_update_slice x0 -> x8, local copies, waits for them, and re-layouts: none -> 22.9 us  [per_device(): lax.dynamic_update_slice_in_dim(returned, placed, (v_next ^ src_i) * earl...]
    all_to_all x1 -> x0, other arithmetic: 19.7 us -> none  [per_device(): lax.all_to_all(projected, 'fourier', split_axis=1, concat_axis=3, tiled=T...]
    all_to_all x1 -> x0, local copies, waits for them, and re-layouts: 16.4 us -> none  [per_device(): lax.all_to_all(projected, 'fourier', split_axis=1, concat_axis=3, tiled=T...]
    add x1 -> x0, other arithmetic: 14.6 us -> none  [per_device(): forcing = velocity + returned]
  transfers between devices with their start and end apart: 5 -> 11, of which waited for: 3 -> 4; matrix products, arithmetic and copies ran while one was open for 5% -> 12% of each run, Pallas kernels for 0% -> 0%
where the time goes in v1:
time: 602 us; the launch traced here: 597 us
  local copies, waits for them, and re-layouts  214 us (36%)
  waiting for transfers between devices  174 us (29%)
  matrix products  124 us (21%)
  other arithmetic  63 us (10%)
  starting transfers between devices  21.4 us (4%)
    ppermute x7, waiting for transfers between devices, per_device(): placed = ppermute(placed, axis_name='fourier', perm=x_next)  101 us
    all_to_all x1, waiting for transfers between devices, per_device(): lax.all_to_all(velocity, 'fourier', split_axis=3, concat_axis=1, tiled=True)  71.2 us
    unnamed x44, local copies, waits for them, and re-layouts  61.2 us
    dynamic_slice x9, local copies, waits for them, and re-layouts, per_device(): lax.dynamic_slice_in_dim(projected, (v_next ^ src_i) * local_next, local_...  39.4 us
    scatter-add x1, other arithmetic, per_device(): jax.ops.segment_sum(values, local_ids, num_segments=owned_count + block_s...  39.3 us
    dot_general x1, matrix products, per_device(): jnp.einsum('ije,fkje->fkie', element_ops, forcing, precision=high)  35.7 us
    all_to_all x3, local copies, waits for them, and re-layouts, per_device(): lax.all_to_all(velocity, 'fourier', split_axis=3, concat_axis=1, tiled=True)  31.7 us
    reshape x2, local copies, waits for them, and re-layouts, per_device(): jnp.transpose(values, (3, 2, 0, 1)).reshape(elems * PERIM, 3 * modes)  24.7 us
  transfers between devices with their start and end apart: 11, of which 4 were waited for; matrix products, arithmetic and copies ran while one was open for 12% of the time, Pallas kernels for 0%

profile of v1, /device:TPU:0, one launch (start us, length us, event | category | flops | bytes accessed | tf_op | source)
XLA Modules:
  0.0 597.1 jit_solution(2658565825616880431)
XLA Ops:
  0.6 12.8 %copy.116 = f32[3,32,64,256]{2,1,0,3:T(8,128)} copy(f32[3,32,64,256]{3,2,1,0:T(8,128)} %param.17) | data formatting | bytes 12582912 | tf_op args[0]
  13.4 12.6 %reshape.114 = f32[8,1,196608]{2,1,0:T(1,128)} reshape(f32[256,3,32,64]{3,2,1,0:T(8,128)} %bitcast.107) | data formatting | bytes 12582912
  26.0 5.3 all-to-all-start
  32.0 71.2 %all-to-all-done = f32[8,1,196608]{2,1,0:T(1,128)} async-done(((f32[8,1,196608]{2,1,0:T(1,128)}), f32[8,1,196608]{2,1,0:T(1,128)}, u32[]{:S(2)}, u32[]{:S(2)}) %all-to-all-start) | async-done | bytes 6291488 | tf_op jit(solution)/shard_map/all_to_all | solution.py:95
  103.7 19.7 %reduce.2 = f32[8,196608]{1,0:T(8,128)} reduce(f32[8,1,196608]{2,1,0:T(1,128)} %all-to-all-done, f32[]{:T(128)} %broadcast.68), dimensions={1}, to_apply=%all_to_all.13.reduce_sub_computation | reduce | bytes 12582916 | tf_op jit(solution)/shard_map/all_to_all | solution.py:95
  123.3 12.2 %reshape.115 = f32[256,3,32,64]{3,2,1,0:T(8,128)} reshape(f32[8,196608]{1,0:T(8,128)} %reduce.2) | data formatting | bytes 12582912
  135.5 20.2 %copy.93 = f32[3,8,32,64,32]{3,4,2,1,0:T(8,128)} copy(f32[3,8,32,64,32]{3,2,0,4,1:T(8,128)} %bitcast.110) | data formatting | bytes 12582912 | tf_op jit(solution)/shard_map/all_to_all | solution.py:95
  155.7 11.0 %copy.94 = f32[3,256,64,32]{1,2,3,0:T(8,128)} copy(f32[3,256,64,32]{2,3,1,0:T(8,128)} %bitcast.111) | data formatting | bytes 12582912 | tf_op jit(solution)/shard_map/all_to_all | solution.py:95
  166.8 13.4 %convolution_bitcast_fusion = f32[3,384,64,32]{1,2,3,0:T(8,128)S(1)} fusion(f32[384,256,1,1]{1,0,3,2:T(8,128)S(1)} %copy-done.8, f32[3,256,64,32]{1,2,3,0:T(8,128)} %copy.94), kind=kOutput, calls=%fused_computation.19 | convolution fusion | flops 7247757312 | bytes 16121856 | tf_op jit(solution)/shard_map/jk,fkpe->fjpe/dot_general | solution.py:96
  180.2 3.7 slice_bitcast_fusion.2
  183.9 2.9 copy-done
  186.7 11.6 %fusion.16 = f32[3,384,32,64]{1,3,2,0:T(8,128)} fusion(f32[3,384,64,32]{1,2,3,0:T(8,128)S(1)} %convolution_bitcast_fusion, f32[64,64,1,1]{1,0,3,2:T(8,128)S(1)} %copy-done.12), kind=kOutput, calls=%fused_computation.56 | convolution fusion | flops 1811939328 | bytes 18890752 | tf_op jit(solution)/shard_map/qp,fjpe->fjqe/dot_general | solution.py:100
  198.4 12.5 %fusion.17 = f32[384,3,64,32]{0,2,3,1:T(8,128)} fusion(f32[384,256,1,1]{1,0,3,2:T(8,128)S(1)} %copy-done.7, f32[3,256,64,32]{1,2,3,0:T(8,128)S(1)} %bitcast.109), kind=kOutput, calls=%fused_computation.57 | convolution fusion | flops 7247757312 | bytes 16121856 | tf_op jit(solution)/shard_map/jk,fkpe->fjpe/dot_general | solution.py:98
  210.9 22.2 %fusion = f32[3,384,64,32]{1,2,3,0:T(8,128)} fusion(f32[3,384,32,64]{1,3,2,0:T(8,128)} %fusion.16, f32[384,3,64,32]{0,2,3,1:T(8,128)} %fusion.17, f32[384,64,32]{0,1,2:T(8,128)} %get-tuple-element.23, f32[64,32]{0,1:T(8,128)S(1)} %copy.98, f32[64,32]{0,1:T(8,128)S(1)} %copy.97, f32[384,64,32]{0,1,2:T(8,128)} %get-tuple-element.24, f32[64,32]{0,1:T(8,128)S(1)} %copy.96, ...), kind=kOutput, calls=%fused_computation.5 | convolution fusion | flops 1840250880 | bytes 47235072 | tf_op jit(solution)/shard_map/qp,fjpe->fjqe/dot_general | solution.py:101
  233.1 18.4 %fusion.6 = f32[3,64,32,256]{3,2,1,0:T(8,128)S(1)} fusion(f32[256,384,1,1]{1,0,3,2:T(8,128)} %constant.107, f32[3,384,64,32]{1,2,3,0:T(8,128)} %fusion), kind=kOutput, calls=%fused_computation.15 | convolution fusion | flops 7247757312 | bytes 16121856 | tf_op jit(solution)/shard_map/kj,fjpe->fkpe/dot_general | solution.py:105
  251.5 12.0 %dynamic-slice_bitcast_fusion = (f32[3,32,64,32]{1,3,2,0:T(8,128)}, f32[3,32,64,32]{1,3,2,0:T(8,128)}, f32[3,32,64,32]{1,3,2,0:T(8,128)}, f32[3,32,64,32]{1,3,2,...) fusion(f32[3,64,32,256]{3,2,1,0:T(8,128)S(1)} %fusion.6, ...), kind=kLoop, calls=%fused_computation.23 | loop fusion | bytes 12582944 | tf_op jit(solution)/shard_map/dynamic_slice | solution.py:116
  263.5 4.0 copy.102
  267.5 2.6 broadcast_multiply_fusion
  270.1 3.8 copy.104
  274.5 2.6 copy.106
  278.4 9.3 %copy.133 = f32[64,64,256,1]{1,0,3,2:T(8,128)} copy(f32[64,64,256,1]{2,1,0,3:T(8,128)} %bitcast.118) | data formatting | bytes 8388608 | tf_op args[3]
  288.0 2.4 copy.101
  290.4 4.0 copy.108
  294.9 3.8 copy.110
  299.8 3.8 copy.112
  303.7 3.0 copy.114
  306.7 6.1 %broadcast_in_dim.15 = f32[3,32,64,256]{2,1,0,3:T(8,128)} broadcast(f32[]{:T(128)} %constant.71.clone.1), dimensions={} | broadcast | bytes 6291460 | tf_op jit(solution)/shard_map/broadcast_in_dim | solution.py:114
  314.6 3.5 copy_dynamic-update-slice_fusion.6
  318.1 2.1 collective-permute-start.6
  320.3 3.5 copy_dynamic-update-slice_fusion.5
  323.8 20.5 %collective-permute-done.2 = f32[3,32,64,32]{2,3,1,0:T(8,128)} collective-permute-done((f32[3,32,64,32]{2,3,1,0:T(8,128)}, f32[3,32,64,32]{2,3,1,0:T(8,128)}, u32[]{:S(2)}, u32[]{:S(2)}) %collective-permute-start.2) | collective-permute-done | bytes 786464 | tf_op jit(solution)/shard_map/ppermute | solution.py:121
  344.4 3.5 copy_dynamic-update-slice_fusion.4
  347.9 3.5 copy_dynamic-update-slice_fusion.3
  351.3 80.4 %collective-permute-done.4 = f32[3,32,64,32]{2,3,1,0:T(8,128)} collective-permute-done((f32[3,32,64,32]{2,3,1,0:T(8,128)}, f32[3,32,64,32]{2,3,1,0:T(8,128)}, u32[]{:S(2)}, u32[]{:S(2)}) %collective-permute-start.4) | collective-permute-done | bytes 786464 | tf_op jit(solution)/shard_map/ppermute | solution.py:121
  431.7 3.5 copy_dynamic-update-slice_fusion.2
  435.2 2.0 copy_dynamic-update-slice_fusion.1
  437.3 2.1 copy_dynamic-update-slice_fusion
  439.4 35.7 %bitcast_add_fusion = f32[3,32,64,256]{2,1,0,3:T(8,128)} fusion(f32[32,64,256]{1,0,2:T(8,128)} %broadcast_multiply_fusion, f32[3,32,64,256]{2,1,0,3:T(8,128)} %copy.116, f32[3,32,64,256]{2,1,0,3:T(8,128)} %copy_dynamic-update-slice_fusion, f32[64,64,256,1]{1,0,3,2:T(8,128)} %copy.133), kind=kOutput, calls=%fused_computation.3 | convolution fusion | flops 1214251008 | bytes 25165824 | tf_op jit(solution)/shard_map/ije,fkje->fkie/dot_general | solution.py:129
  475.1 12.1 %copy.120 = f32[3,32,64,256]{3,1,0,2:T(8,128)} copy(f32[3,32,64,256]{2,1,0,3:T(8,128)} %bitcast_add_fusion) | data formatting | bytes 12582912 | tf_op jit(solution)/shard_map/add | solution.py:130
  487.2 3.5 gather_fusion
  490.7 10.0 %copy.138 = f32[256,28,3,32]{3,2,1,0:T(4,128)} copy(f32[256,28,3,32]{0,3,2,1:T(8,128)S(1)} %bitcast.113) | data formatting | bytes 5505024 | tf_op jit(solution)/shard_map/reshape | solution.py:133
  500.7 14.7 %reshape.111 = f32[7168,96]{1,0:T(8,128)} reshape(f32[256,28,3,32]{3,2,1,0:T(4,128)} %copy.138) | data formatting | bytes 5505024 | tf_op jit(solution)/shard_map/reshape | solution.py:133
  515.4 39.3 %scatter_custom_fusion = f32[3456,96]{1,0:T(8,128)S(1)} fusion(s32[7168]{0:T(1024)S(1)} %reshape.95, f32[7168,96]{1,0:T(8,128)} %reshape.111, f32[]{:T(128)} %constant.71.clone.1), kind=kCustom, calls=%fused_computation.41 | custom fusion | flops 688128 | bytes 1327616 | tf_op jit(solution)/shard_map/scatter-add | solution.py:135
  555.3 4.3 collective-permute-start.7
  561.4 4.2 collective-permute-start.8
  566.9 11.2 %copy.127 = f32[3,32,64,256]{3,2,1,0:T(8,128)} copy(f32[3,32,64,256]{2,1,0,3:T(8,128)} %bitcast_add_fusion) | data formatting | bytes 12582912
  581.9 3.2 gather_fusion.1
  585.0 9.8 %convolution_bitcast_fusion.1 = f32[96,26,128]{2,0,1:T(8,128)S(1)} fusion(f32[96,26,4,128]{3,0,2,1:T(8,128)} %bitcast.112, f32[26,4,128,128]{3,2,1,0:T(8,128)} %param.23), kind=kOutput, calls=%fused_computation.40 | convolution fusion | flops 1962934272 | bytes 13205504 | tf_op jit(solution)/shard_map/rsab,frsb->fra/dot_general | solution.py:146
  (80 shorter events, 16.1 us)
Async XLA Ops:
  26.0 5.3 copy-start.10
  26.0 5.7 copy-start.9
  26.0 5.9 copy-start.16
  26.0 77.1 %all-to-all-start = ((f32[8,1,196608]{2,1,0:T(1,128)}), f32[8,1,196608]{2,1,0:T(1,128)}, u32[]{:S(2)}, u32[]{:S(2)}) async-start(f32[8,1,196608]{2,1,0:T(1,128)} %reshape.114), calls=%async_computation | async-start | bytes 12582912 | tf_op jit(solution)/shard_map/all_to_all | solution.py:95
  155.7 11.0 %copy-start.8 = (f32[384,256,1,1]{1,0,3,2:T(8,128)S(1)}, f32[384,256,1,1]{1,0,3,2:T(8,128)}, u32[]{:S(2)}) copy-start(f32[384,256,1,1]{1,0,3,2:T(8,128)} %constant.103) | copy-start | bytes 1179652
  180.2 6.6 %copy-start = (f32[3,384,64,32]{1,2,3,0:T(8,128)}, f32[3,384,64,32]{1,2,3,0:T(8,128)S(1)}, u32[]{:S(2)}) copy-start(f32[3,384,64,32]{1,2,3,0:T(8,128)S(1)} %convolution_bitcast_fusion) | copy-start | bytes 28311556
  180.2 6.6 %copy-start.12 = (f32[64,64,1,1]{1,0,3,2:T(8,128)S(1)}, f32[64,64,1,1]{1,0,3,2:T(8,128)}, u32[]{:S(2)}) copy-start(f32[64,64,1,1]{1,0,3,2:T(8,128)} %constant.104) | copy-start | bytes 49156
  180.2 18.2 %slice-start = ((s8[6291456]{0:T(1024)(128)(4,1)}), s8[4194304]{0:T(1024)(128)(4,1)S(1)}, s32[]{:S(2)}) async-start(s8[6291456]{0:T(1024)(128)(4,1)} %bitcast.108), calls=%async_computation.1 | async-start | bytes 8388608
  186.7 11.6 %slice-start.1 = ((s8[6291456]{0:T(1024)(128)(4,1)}), s8[2097152]{0:T(1024)(128)(4,1)S(1)}, s32[]{:S(2)}) async-start(s8[6291456]{0:T(1024)(128)(4,1)} %bitcast.108), calls=%async_computation.2 | async-start | bytes 4194304
  186.7 11.6 %copy-start.7 = (f32[384,256,1,1]{1,0,3,2:T(8,128)S(1)}, f32[384,256,1,1]{1,0,3,2:T(8,128)}, u32[]{:S(2)}) copy-start(f32[384,256,1,1]{1,0,3,2:T(8,128)} %constant.106) | copy-start | bytes 1179652
  198.4 12.5 %copy-start.11 = (f32[64,64,1,1]{1,0,3,2:T(8,128)S(1)}, f32[64,64,1,1]{1,0,3,2:T(8,128)}, u32[]{:S(2)}) copy-start(f32[64,64,1,1]{1,0,3,2:T(8,128)} %constant.105) | copy-start | bytes 49156
  263.4 11.0 %copy-start.13 = (s32[256,28]{0,1:T(8,128)S(1)}, s32[256,28]{0,1:T(8,128)}, u32[]{:S(2)}) copy-start(s32[256,28]{0,1:T(8,128)} %param.21) | copy-start | bytes 86020
  263.4 11.0 %copy-start.3 = (f32[3,32,64,32]{1,3,2,0:T(8,128)S(1)}, f32[3,32,64,32]{1,3,2,0:T(8,128)}, u32[]{:S(2)}) copy-start(f32[3,32,64,32]{1,3,2,0:T(8,128)} %get-tuple-element.29) | copy-start | bytes 2359300
  267.5 11.0 %copy-start.15 = (s32[28]{0:T(128)S(1)}, s32[28]{0:T(128)}, u32[]{:S(2)}) copy-start(s32[28]{0:T(128)} %constant.102) | copy-start | bytes 340
  267.5 46.6 %collective-permute-start = (f32[3,32,64,32]{2,3,1,0:T(8,128)}, f32[3,32,64,32]{2,3,1,0:T(8,128)}, u32[]{:S(2)}, u32[]{:S(2)}) collective-permute-start(f32[3,32,64,32]{2,3,1,0:T(8,128)} %copy.102), channel_id=1, source_target_pairs={{0,4},{4,0},{8,12},{12,8},{16,20},{20,16},{24,28},{28,24},{1,5},{5... | collective-permute-start | bytes 2359304 | tf_op jit(solution)/shard_map/ppermute | solution.py:121
  273.9 44.2 %collective-permute-start.1 = (f32[3,32,64,32]{2,3,1,0:T(8,128)}, f32[3,32,64,32]{2,3,1,0:T(8,128)}, u32[]{:S(2)}, u32[]{:S(2)}) collective-permute-start(f32[3,32,64,32]{2,3,1,0:T(8,128)} %copy.104), channel_id=1, source_target_pairs={{0,8},{4,12},{8,0},{12,4},{16,24},{20,28},{24,16},{28,20},{1,9},{5... | collective-permute-start | bytes 2359304 | tf_op jit(solution)/shard_map/ppermute | solution.py:121
  277.1 67.3 %collective-permute-start.2 = (f32[3,32,64,32]{2,3,1,0:T(8,128)}, f32[3,32,64,32]{2,3,1,0:T(8,128)}, u32[]{:S(2)}, u32[]{:S(2)}) collective-permute-start(f32[3,32,64,32]{2,3,1,0:T(8,128)} %copy.106), channel_id=1, source_target_pairs={{0,12},{4,8},{8,4},{12,0},{16,28},{20,24},{24,20},{28,16},{1,13},{... | collective-permute-start | bytes 2359304 | tf_op jit(solution)/shard_map/ppermute | solution.py:121
  278.4 9.6 %copy-start.2 = (f32[3,32,64,32]{1,3,2,0:T(8,128)S(1)}, f32[3,32,64,32]{1,3,2,0:T(8,128)}, u32[]{:S(2)}) copy-start(f32[3,32,64,32]{1,3,2,0:T(8,128)} %get-tuple-element.32) | copy-start | bytes 2359300
  290.4 13.3 %copy-start.1 = (f32[3,32,64,32]{1,3,2,0:T(8,128)S(1)}, f32[3,32,64,32]{1,3,2,0:T(8,128)}, u32[]{:S(2)}) copy-start(f32[3,32,64,32]{1,3,2,0:T(8,128)} %get-tuple-element.25) | copy-start | bytes 2359300
  294.4 53.5 %collective-permute-start.3 = (f32[3,32,64,32]{2,3,1,0:T(8,128)}, f32[3,32,64,32]{2,3,1,0:T(8,128)}, u32[]{:S(2)}, u32[]{:S(2)}) collective-permute-start(f32[3,32,64,32]{2,3,1,0:T(8,128)} %copy.108), channel_id=1, source_target_pairs={{0,16},{4,20},{8,24},{12,28},{16,0},{20,4},{24,8},{28,12},{1,17},{... | collective-permute-start | bytes 2359304 | tf_op jit(solution)/shard_map/ppermute | solution.py:121
  298.7 133.0 %collective-permute-start.4 = (f32[3,32,64,32]{2,3,1,0:T(8,128)}, f32[3,32,64,32]{2,3,1,0:T(8,128)}, u32[]{:S(2)}, u32[]{:S(2)}) collective-permute-start(f32[3,32,64,32]{2,3,1,0:T(8,128)} %copy.110), channel_id=1, source_target_pairs={{0,20},{4,16},{8,28},{12,24},{16,4},{20,0},{24,12},{28,8},{1,21},{... | collective-permute-start | bytes 2359304 | tf_op jit(solution)/shard_map/ppermute | solution.py:121
  306.7 6.1 %copy-start.4 = (f32[3,32,64,32]{2,1,0,3:T(8,128)S(1)}, f32[3,32,64,32]{2,1,0,3:T(8,128)}, u32[]{:S(2)}) copy-start(f32[3,32,64,32]{2,1,0,3:T(8,128)} %copy.101) | copy-start | bytes 2359300
  306.7 7.4 %copy-start.6 = (f32[3,32,64,32]{2,3,1,0:T(8,128)S(1)}, f32[3,32,64,32]{2,3,1,0:T(8,128)}, u32[]{:S(2)}) copy-start(f32[3,32,64,32]{2,3,1,0:T(8,128)} %copy.112) | copy-start | bytes 2359300
  312.8 5.3 copy-start.5
  314.1 121.2 %collective-permute-start.5 = (f32[3,32,64,32]{2,3,1,0:T(8,128)S(1)}, f32[3,32,64,32]{2,3,1,0:T(8,128)S(1)}, u32[]{:S(2)}, u32[]{:S(2)}) collective-permute-start(f32[3,32,64,32]{2,3,1,0:T(8,128)S(1)} %copy-done.6), channel_id=1, source_target_pairs={{0,24},{4,28},{8,16},{12,20},{16,8},{20,12},{24,0},{28,4},{1,25},{... | collective-permute-start | bytes 2359304 | tf_op jit(solution)/shard_map/ppermute | solution.py:121
  318.1 119.2 %collective-permute-start.6 = (f32[3,32,64,32]{2,3,1,0:T(8,128)S(1)}, f32[3,32,64,32]{2,3,1,0:T(8,128)S(1)}, u32[]{:S(2)}, u32[]{:S(2)}) collective-permute-start(f32[3,32,64,32]{2,3,1,0:T(8,128)S(1)} %copy-done.5), channel_id=1, source_target_pairs={{0,28},{4,24},{8,20},{12,16},{16,12},{20,8},{24,4},{28,0},{1,29},{... | collective-permute-start | bytes 2359304 | tf_op jit(solution)/shard_map/ppermute | solution.py:121
  500.7 58.9 %copy-start.14 = (s32[26,4]{0,1:T(4,128)S(1)}, s32[26,4]{0,1:T(4,128)}, u32[]{:S(2)}) copy-start(s32[26,4]{0,1:T(4,128)} %param.22) | copy-start | bytes 1252
  555.3 6.1 %collective-permute-start.7 = (f32[3,32,128]{2,1,0:T(8,128)S(1)}, f32[3,32,128]{2,1,0:T(8,128)S(1)}, u32[]{:S(2)}, u32[]{:S(2)}) collective-permute-start(f32[3,32,128]{2,1,0:T(8,128)S(1)} %slice.79), channel_id=1, source_target_pairs={{0,1},{1,2},{2,3},{4,5},{5,6},{6,7},{8,9},{9,10},{10,11},{12,13},{... | collective-permute-start | bytes 147464 | tf_op jit(solution)/shard_map/ppermute | solution.py:27
  561.4 16.8 %collective-permute-start.8 = (f32[3,32,256]{2,1,0:T(8,128)S(1)}, f32[3,32,256]{2,1,0:T(8,128)S(1)}, u32[]{:S(2)}, u32[]{:S(2)}) collective-permute-start(f32[3,32,256]{2,1,0:T(8,128)S(1)} %get-tuple-element.33), channel_id=1, source_target_pairs={{0,1},{1,2},{2,3},{4,5},{5,6},{6,7},{8,9},{9,10},{10,11},{12,13},{... | collective-permute-start | bytes 294920 | tf_op jit(solution)/shard_map/ppermute | solution.py:37
  565.6 12.5 %collective-permute-start.9 = (f32[3,32,256]{2,1,0:T(8,128)S(1)}, f32[3,32,256]{2,1,0:T(8,128)S(1)}, u32[]{:S(2)}, u32[]{:S(2)}) collective-permute-start(f32[3,32,256]{2,1,0:T(8,128)S(1)} %get-tuple-element.34), channel_id=1, source_target_pairs={{1,0},{2,1},{3,2},{5,4},{6,5},{7,6},{9,8},{10,9},{11,10},{13,12},{... | collective-permute-start | bytes 294920 | tf_op jit(solution)/shard_map/ppermute | solution.py:38
